TPU v7x, 512 devices: a whole 4x4x16 slice. The times are simulated.
512 devices in a mesh: pair: 128 (over z, x, core), red: 4 (over y).
Axes of the slice: x: 4, y: 4, z: 16, core: 2. Of those that a mesh axis runs over, the one named last changes fastest.
Arguments:
- amplitudes: bfloat16 [256, 128, 1024], P('pair', None, 'red'), may hold values from -6 to 6
- ladder_ints: bfloat16 [128, 1024, 1024], P('pair', 'red'), may hold values from -0.25 to 0.25
- live_count: int32 [128], replicated, may hold values from 128 to 1024, as said below
Outputs:
- residual: bfloat16 [256, 128, 1024], P('pair', None, 'red')
Inputs may be any that keep to these rules, and one draw needn't show every extreme that they name: Only contracted pairs c < live_count[s] of slab s take part; in every draw some slab has all 1024 pairs live.
All inputs are finite; a program needn't handle non-finite values.
Results may differ from a plain program's by a relative error of at most 0.012.
Values may be sent and summed in bfloat16 or wider, within the bound.
A program may use at most 128 MiB of HBM per device.

v0:
```python
import jax
import jax.numpy as jnp
from jax import lax
from jax.sharding import PartitionSpec as P


def reduce_shares(partial_value):
    share_width = partial_value.shape[2] // lax.axis_size("red")
    summed = lax.psum(partial_value.astype(jnp.bfloat16), "red").astype(jnp.float32)
    return lax.dynamic_slice_in_dim(summed, lax.axis_index("red") * share_width, share_width, 2)


def body(amplitudes, ladder_ints, live_count):
    slab_index = lax.axis_index("pair")
    share_index = lax.axis_index("red")
    regrouped = lax.all_to_all(amplitudes, "pair", split_axis=1, concat_axis=0, tiled=True)
    block = regrouped[:, 0, :]
    share_width = block.shape[1]
    slab_count = live_count.shape[0]
    live_limit = jnp.sum(
        jnp.where(jnp.arange(slab_count, dtype=jnp.int32) == slab_index, live_count, 0)
    )
    position = share_index * share_width + jnp.arange(share_width, dtype=jnp.int32)
    masked = jnp.where(position[None, :] < live_limit, block, jnp.zeros_like(block))
    partial_value = jnp.dot(masked, ladder_ints[0], preferred_element_type=jnp.float32)
    partial_value = partial_value[:, None, :]
    moved = lax.all_to_all(
        partial_value.astype(jnp.bfloat16), "pair", split_axis=0, concat_axis=1, tiled=True
    )
    return reduce_shares(moved.astype(jnp.float32)).astype(jnp.bfloat16)


def solution(mesh):
    in_specs = (P("pair", None, "red"), P("pair", "red", None), P())
    out_specs = P("pair", None, "red")
    return jax.shard_map(body, mesh=mesh, in_specs=in_specs, out_specs=out_specs, check_vma=False)
```

profile of v0, /device:TPU:2, one launch (start us, length us, event | category | flops | bytes accessed | tf_op | source)
XLA Modules:
  0.0 149.6 jit_solution(17337359764642066357)
XLA Ops:
  6.5 0.0 copy-start
  6.5 1.8 %copy.10 = bf16[2,128,256]{2,0,1:T(2,128)(2,1)} copy(bf16[2,128,256]{2,1,0:T(8,128)(2,1)} %param.3) | data formatting | bytes 262144 | tf_op args[0]
  8.3 19.4 %all-to-all-start = ((bf16[2,128,256]{2,0,1:T(2,128)(2,1)}), bf16[2,128,256]{2,0,1:T(2,128)(2,1)S(1)}, u32[]{:S(2)}, u32[]{:S(2)}) async-start(bf16[2,128,256]{2,0,1:T(2,128)(2,1)} %copy.10), calls=%async_computation | async-start | bytes 262144 | tf_op jit(solution)/shard_map/all_to_all | solution.py:16
  27.7 0.0 all-reduce.2.cloned.1.call-start
  27.8 0.0 copy-start.1
  27.8 0.6 copy-done.1
  28.4 0.7 fusion.3
  29.1 0.7 add_compare_fusion
  29.8 14.0 %all-to-all-done = bf16[2,128,256]{2,0,1:T(2,128)(2,1)S(1)} async-done(((bf16[2,128,256]{2,0,1:T(2,128)(2,1)}), bf16[2,128,256]{2,0,1:T(2,128)(2,1)S(1)}, u32[]{:S(2)}, u32[]{:S(2)}) %all-to-all-start) | async-done | bytes 131104 | tf_op jit(solution)/shard_map/all_to_all | solution.py:16
  43.8 0.1 fusion.2
  43.9 0.1 select_n.20
  44.0 0.0 copy-done
  44.0 0.3 fusion
  44.3 0.5 broadcast.20
  44.8 1.0 reduce.1
  45.9 0.2 reshape.16
  46.1 38.2 %all_to_all.30 = bf16[128,2,1024]{2,1,0:T(2,128)(2,1)S(1)} all-to-all(bf16[128,2,1024]{2,1,0:T(2,128)(2,1)S(1)} %reshape.16), channel_id=1, replica_groups=mesh['pair'=128,'red'=4] {'pair'}, dimensions={0} | all-to-all | bytes 1048576 | tf_op jit(solution)/shard_map/all_to_all | solution.py:27
  84.3 0.4 reshape.17
  84.8 3.1 %reduce = bf16[256,1024]{1,0:T(8,128)(2,1)S(1)} reduce(bf16[256,1,1024]{2,1,0:T(2,128)(2,1)S(1)} %reshape.17, bf16[]{:T(256)} %constant.19), dimensions={1}, to_apply=%all_to_all.24.reduce_sub_computation | reduce | bytes 1048578 | tf_op jit(solution)/shard_map/all_to_all | solution.py:27
  87.8 1.0 all_to_all.25
  88.8 0.0 all-reduce.2.cloned.1.call-update
  88.9 52.2 %all-reduce.2.cloned.1.call-done = bf16[2,128,1024]{2,0,1:T(2,128)(2,1)} async-done(((bf16[2,128,1024]{2,0,1:T(2,128)(2,1)}), bf16[2,128,1024]{2,0,1:T(2,128)(2,1)}) %all-reduce.2.cloned.1.call-update) | async-done | bytes 524304 | tf_op jit(solution)/shard_map/psum | solution.py:9
  141.1 1.0 convert_convert_fusion
  142.1 0.7 copy.12
Async XLA Ops:
  6.5 37.5 %copy-start = (bf16[1,256,1024]{2,1,0:T(8,128)(2,1)S(1)}, bf16[1,256,1024]{2,1,0:T(8,128)(2,1)}, u32[]{:S(2)}) copy-start(bf16[1,256,1024]{2,1,0:T(8,128)(2,1)} %param.4) | copy-start | bytes 1572868
  8.3 35.5 %all-to-all-start = ((bf16[2,128,256]{2,0,1:T(2,128)(2,1)}), bf16[2,128,256]{2,0,1:T(2,128)(2,1)S(1)}, u32[]{:S(2)}, u32[]{:S(2)}) async-start(bf16[2,128,256]{2,0,1:T(2,128)(2,1)} %copy.10), calls=%async_computation | async-start | bytes 262144 | tf_op jit(solution)/shard_map/all_to_all | solution.py:16
  27.7 113.4 %all-reduce.2.cloned.1.call-start = ((), (), s32[]{:S(2)}) async-start(), calls=%async_computation.2 | async-start | bytes 1048576 | tf_op jit(solution)/shard_map/psum | solution.py:9
  27.8 0.7 copy-start.1
Sparse Core Ops, SparseCore 0:
  89.0 52.0 all-reduce.1
where the time goes:
time: 150 us
  waiting for transfers between devices  66.2 us (44%)
  blocking collectives  38.2 us (25%)
  starting transfers between devices  19.5 us (13%)
  between operations  13.5 us (9%)
  other arithmetic  6.59 us (4%)
  local copies, waits for them, and re-layouts  5.29 us (4%)
    psum x1, waiting for transfers between devices, reduce_shares(): lax.psum(partial_value.astype(jnp.bfloat16), 'red').astype(jnp.float32)  52.2 us
    all_to_all x1, blocking collectives, body(): lax.all_to_all(partial_value.astype(jnp.bfloat16), 'pair', split_axis=0,...  38.2 us
    all_to_all x1, starting transfers between devices, body(): lax.all_to_all(amplitudes, 'pair', split_axis=1, concat_axis=0, tiled=True)  19.4 us
    all_to_all x1, waiting for transfers between devices, body(): lax.all_to_all(amplitudes, 'pair', split_axis=1, concat_axis=0, tiled=True)  14 us
    all_to_all x1, other arithmetic, body(): lax.all_to_all(partial_value.astype(jnp.bfloat16), 'pair', split_axis=0,...  3.05 us
    unnamed x7, local copies, waits for them, and re-layouts  3.04 us
  transfers between devices with their start and end apart: 2, of which 2 were waited for; matrix products, arithmetic and copies ran while one was open for 1% of the time, Pallas kernels for 0%

commit v1 on v0

--- a/solution.py
+++ b/solution.py
@@ -6,7 +6,9 @@
 
 def reduce_shares(partial_value):
     share_width = partial_value.shape[2] // lax.axis_size("red")
-    summed = lax.psum(partial_value.astype(jnp.bfloat16), "red").astype(jnp.float32)
+    summed = jnp.sum(lax.all_gather(partial_value.astype(jnp.bfloat16), "red"), axis=0).astype(
+        jnp.float32
+    )
     return lax.dynamic_slice_in_dim(summed, lax.axis_index("red") * share_width, share_width, 2)
 
 

time: 150 us -> 132 us (0.88)
  the two profiles are of different devices: /device:TPU:2 before, /device:TPU:1 now
where the time goes in v1:
time: 132 us
  waiting for transfers between devices  46.7 us (35%)
  blocking collectives  37.8 us (29%)
  starting transfers between devices  20.4 us (15%)
  between operations  13.5 us (10%)
  other arithmetic  8.96 us (7%)
  local copies, waits for them, and re-layouts  4.08 us (3%)
    all_to_all x1, blocking collectives, body(): lax.all_to_all(partial_value.astype(jnp.bfloat16), 'pair', split_axis=0,...  37.8 us
    all_gather x1, waiting for transfers between devices, reduce_shares(): lax.all_gather(partial_value.astype(jnp.bfloat16), 'red')  32.7 us
    all_to_all x1, starting transfers between devices, body(): lax.all_to_all(amplitudes, 'pair', split_axis=1, concat_axis=0, tiled=True)  20.4 us
    all_to_all x1, waiting for transfers between devices, body(): lax.all_to_all(amplitudes, 'pair', split_axis=1, concat_axis=0, tiled=True)  13.9 us
    all_to_all x1, other arithmetic, body(): lax.all_to_all(partial_value.astype(jnp.bfloat16), 'pair', split_axis=0,...  3.05 us
  transfers between devices with their start and end apart: 2, of which 2 were waited for; matrix products, arithmetic and copies ran while one was open for 2% of the time, Pallas kernels for 0%

profile of v1, /device:TPU:1, one launch (start us, length us, event | category | flops | bytes accessed | tf_op | source)
XLA Modules:
  0.0 131.7 jit_solution(17623530798297701056)
XLA Ops:
  6.5 0.0 copy-start
  6.5 1.8 %copy.10 = bf16[2,128,256]{2,0,1:T(2,128)(2,1)} copy(bf16[2,128,256]{2,1,0:T(8,128)(2,1)} %param.3) | data formatting | bytes 262144 | tf_op args[0]
  8.3 20.4 %all-to-all-start = ((bf16[2,128,256]{2,0,1:T(2,128)(2,1)}), bf16[2,128,256]{2,0,1:T(2,128)(2,1)S(1)}, u32[]{:S(2)}, u32[]{:S(2)}) async-start(bf16[2,128,256]{2,0,1:T(2,128)(2,1)} %copy.10), calls=%async_computation | async-start | bytes 262144 | tf_op jit(solution)/shard_map/all_to_all | solution.py:18
  28.7 0.0 all-gather.3.cloned.1.call-start
  28.7 1.4 %fusion.3 = s32[]{:T(128)} fusion(s32[128]{0:T(128)} %param.5, s32[]{:T(128)S(6)} %axis_index.29), kind=kLoop, calls=%fused_computation.8 | loop fusion | flops 383 | bytes 520 | tf_op jit(solution)/shard_map/reduce_sum | solution.py:22
  30.1 0.7 add_compare_fusion
  30.8 13.9 %all-to-all-done = bf16[2,128,256]{2,0,1:T(2,128)(2,1)S(1)} async-done(((bf16[2,128,256]{2,0,1:T(2,128)(2,1)}), bf16[2,128,256]{2,0,1:T(2,128)(2,1)S(1)}, u32[]{:S(2)}, u32[]{:S(2)}) %all-to-all-start) | async-done | bytes 131104 | tf_op jit(solution)/shard_map/all_to_all | solution.py:18
  44.8 0.1 fusion.2
  44.9 0.1 select_n.20
  44.9 0.0 copy-done
  44.9 0.3 fusion
  45.2 0.5 broadcast.20
  45.8 1.0 reduce.2
  46.8 0.2 reshape.18
  47.0 37.8 %all_to_all.27 = bf16[128,2,1024]{2,1,0:T(2,128)(2,1)S(1)} all-to-all(bf16[128,2,1024]{2,1,0:T(2,128)(2,1)S(1)} %reshape.18), channel_id=1, replica_groups=mesh['pair'=128,'red'=4] {'pair'}, dimensions={0} | all-to-all | bytes 1048576 | tf_op jit(solution)/shard_map/all_to_all | solution.py:29
  84.8 0.4 reshape.19
  85.2 3.1 %reduce.1 = bf16[256,1024]{1,0:T(8,128)(2,1)S(1)} reduce(bf16[256,1,1024]{2,1,0:T(2,128)(2,1)S(1)} %reshape.19, bf16[]{:T(256)} %constant.21), dimensions={1}, to_apply=%all_to_all.22.reduce_sub_computation | reduce | bytes 1048578 | tf_op jit(solution)/shard_map/all_to_all | solution.py:29
  88.3 0.2 all_to_all.23
  88.5 0.9 copy.12
  89.4 0.0 all-gather.3.cloned.1.call-update
  89.4 32.7 %all-gather.3.cloned.1.call-done = bf16[8,128,1,1024]{3,1,2,0:T(8,128)(2,1)} async-done(((bf16[2,128,1,1024]{3,1,2,0:T(8,128)(2,1)}), bf16[8,128,1,1024]{3,1,2,0:T(8,128)(2,1)}) %all-gather.3.cloned.1.call-update) | async-done | bytes 2097168 | tf_op jit(solution)/shard_map/all_gather | solution.py:9
  122.1 2.0 %reduce_sum.22 = bf16[2,128,1024]{2,1,0:T(8,128)(2,1)S(1)} reduce(bf16[4,2,128,1024]{3,2,1,0:T(8,128)(2,1)} %bitcast.14, bf16[]{:T(256)} %constant.17.clone.1), dimensions={0}, to_apply=%region_1.2 | reduce | flops 786432 | bytes 2621442 | tf_op jit(solution)/shard_map/reduce_sum | solution.py:9
  124.2 0.7 convert_convert_fusion
Async XLA Ops:
  6.5 38.4 %copy-start = (bf16[1,256,1024]{2,1,0:T(8,128)(2,1)S(1)}, bf16[1,256,1024]{2,1,0:T(8,128)(2,1)}, u32[]{:S(2)}) copy-start(bf16[1,256,1024]{2,1,0:T(8,128)(2,1)} %param.4) | copy-start | bytes 1572868
  8.3 36.5 %all-to-all-start = ((bf16[2,128,256]{2,0,1:T(2,128)(2,1)}), bf16[2,128,256]{2,0,1:T(2,128)(2,1)S(1)}, u32[]{:S(2)}, u32[]{:S(2)}) async-start(bf16[2,128,256]{2,0,1:T(2,128)(2,1)} %copy.10), calls=%async_computation | async-start | bytes 262144 | tf_op jit(solution)/shard_map/all_to_all | solution.py:18
  28.7 93.5 %all-gather.3.cloned.1.call-start = ((), (), s32[]{:S(2)}) async-start(), calls=%async_computation.2 | async-start | bytes 2621440 | tf_op jit(solution)/shard_map/all_gather | solution.py:9
Sparse Core Ops, SparseCore 0:
  89.6 32.5 all-gather.2
